TPU v7x, 32 devices: a whole 2x2x4 slice. The times are simulated.
32 devices in a mesh: grp: 2 (over x), head: 16 (over z, y, core).
Axes of the slice: x: 2, y: 2, z: 4, core: 2. Of those that a mesh axis runs over, the one named last changes fastest.
Arguments:
- queries: bfloat16 [2048, 2, 16, 256], P('head', 'grp'), parts along dimension 1, may hold values from -12 to 12
- new_kv: bfloat16 [2048, 2, 2, 512], P('head', 'grp'), parts along dimension 1, may hold values from -4 to 4
- cache: bfloat16 [32, 256, 512], P(('grp', 'head')), parts along dimension 0, may hold values from -12 to 12
- resid: bfloat16 [2048, 2, 2048], P('head', 'grp'), parts along dimension 1, may hold values from -6 to 6
- w_out: bfloat16 [16, 256, 2048], P(None, 'head'), may hold values from -0.375 to 0.375
- norm_gain: float32 [2048], replicated, may hold values from 0.1 to 1.9
- expert_ids: int32 [2048, 2, 2], P('head', 'grp'), parts along dimension 1, may hold values from 0 to 15, all different within a row; in each aligned block of 128 rows (0 to 127, 128 to 255, ..., all dimensions but the last counted through in order) at most 32 rows name the same one
- expert_gates: float32 [2048, 2, 2], P('head', 'grp'), parts along dimension 1, may hold values from 0.2 to 1
- w_in: bfloat16 [16, 2048, 1024], P('head'), may hold values from -0.125 to 0.125
- w_down: bfloat16 [16, 512, 2048], P('head'), may hold values from -0.25 to 0.25
Outputs:
- layer_out: bfloat16 [2048, 2, 2048], P('head', 'grp'), parts along dimension 1
There are 2 independent parts, one for each index of `grp`. A program takes and returns all parts, laid end to end along the dimension named above; an argument that names none is the same for every part. Nothing has to cross between parts.
Inputs may be any that keep to these rules, and one draw needn't show every extreme that they name: `expert_ids`: rows are taken in order over positions and then sequences; in each aligned block of 128 such rows (the rows of one device) no expert is named by more than 32 rows, a bound that some block reaches. A row names 2 different experts.
All inputs are finite; a program needn't handle non-finite values.
Results may differ from a plain program's by a relative error of at most 0.009.
Values may be sent and summed in bfloat16 or wider, within the bound.
A program may use at most 128 MiB of HBM per device.

v0:
```python
import jax
import jax.numpy as jnp
from jax import lax
from jax.sharding import PartitionSpec as P

eps_norm = 1e-06


def partner_2(value, axis, stride):
    mask = 2**stride
    pairs = [(source, source ^ mask) for source in range(lax.axis_size(axis))]
    return lax.ppermute(value, axis, pairs)


def attend(query_rows_all, new_keys, new_values, cached):
    length = query_rows_all.shape[0]
    head_width = query_rows_all.shape[1]
    block_rows = min(512, length)
    score_scale = head_width ** (-0.5)
    old_keys = cached[:, :head_width]
    old_values = cached[:, head_width:]
    key_positions = jnp.arange(length, dtype=jnp.int32)

    def one_block(first_row):
        query_rows = lax.dynamic_slice_in_dim(query_rows_all, first_row, block_rows, 0)
        old_scores = (
            jnp.dot(query_rows, old_keys.T, preferred_element_type=jnp.float32) * score_scale
        )
        new_scores = (
            jnp.dot(query_rows, new_keys.T, preferred_element_type=jnp.float32) * score_scale
        )
        row_positions = first_row + jnp.arange(block_rows, dtype=jnp.int32)
        allowed = key_positions[None, :] <= row_positions[:, None]
        new_scores = jnp.where(allowed, new_scores, -jnp.inf)
        row_max = jnp.maximum(jnp.max(old_scores, 1), jnp.max(new_scores, 1))[:, None]
        old_exp = jnp.exp(old_scores - row_max)
        new_exp = jnp.exp(new_scores - row_max)
        denominator = jnp.sum(old_exp, 1) + jnp.sum(new_exp, 1)
        weighted_sum = jnp.dot(
            old_exp.astype(jnp.bfloat16), old_values, preferred_element_type=jnp.float32
        )
        weighted_sum = weighted_sum + jnp.dot(
            new_exp.astype(jnp.bfloat16), new_values, preferred_element_type=jnp.float32
        )
        return (weighted_sum / denominator[:, None]).astype(jnp.bfloat16)

    starts = jnp.arange(length // block_rows) * block_rows
    return lax.map(one_block, starts).reshape(length, head_width)


def local(queries, new_kv, cache, resid, w_out, norm_gain, expert_ids, expert_gates, w_in, w_down):
    axis_count = lax.axis_size("head")
    local_rows = queries.shape[0]
    seq_count = queries.shape[1]
    head_count = queries.shape[2]
    head_width = queries.shape[3]
    pair_heads = new_kv.shape[2]
    group_size = head_count // pair_heads
    model_width = resid.shape[2]
    row_count = local_rows * seq_count
    query_slots = queries.reshape(local_rows, axis_count, head_width)
    pair_slots = jnp.broadcast_to(
        new_kv[:, :, :, None, :], (local_rows, seq_count, pair_heads, group_size, 2 * head_width)
    )
    pair_slots = pair_slots.reshape(local_rows, axis_count, 2 * head_width)
    head_queries = lax.all_to_all(query_slots, "head", split_axis=1, concat_axis=0, tiled=True)[
        :, 0
    ]
    head_pairs = lax.all_to_all(pair_slots, "head", split_axis=1, concat_axis=0, tiled=True)[:, 0]
    cache_rows = cache[0]
    for bit_number in range(group_size.bit_length() - 1):
        partner = partner_2(cache_rows, "head", bit_number)
        cache_rows = jnp.concatenate([cache_rows, partner], 0)
    attended = attend(
        head_queries, head_pairs[:, :head_width], head_pairs[:, head_width:], cache_rows
    )
    returned = lax.all_to_all(
        attended.reshape(attended.shape[0], 1, head_width),
        "head",
        split_axis=0,
        concat_axis=1,
        tiled=True,
    )
    attn_rows = returned.reshape(row_count, head_count * head_width)
    attn_heads = attn_rows.reshape(row_count, head_count, head_width)
    projected = jnp.einsum(
        "rhi,hid->rd",
        attn_heads,
        lax.all_gather(w_out, "head", axis=1, tiled=True),
        preferred_element_type=jnp.float32,
    )
    stream = resid.reshape(row_count, model_width).astype(jnp.float32) + projected
    normed = stream * lax.rsqrt(jnp.mean(stream * stream, 1, keepdims=True) + eps_norm) * norm_gain
    normed = normed.astype(jnp.bfloat16)
    top_count = expert_ids.shape[2]
    flat_ids = expert_ids.reshape(-1)
    local_experts = w_in.shape[0]
    experts = local_experts * axis_count
    capacity = max(2, 2 * row_count * top_count // experts)
    onehot = (flat_ids[:, None] == jnp.arange(experts, dtype=jnp.int32)[None, :]).astype(jnp.int32)
    earlier = jnp.cumsum(onehot, 0) - onehot
    slot_rank = jnp.sum(earlier * onehot, 1)
    target = flat_ids * capacity + slot_rank
    repeated = jnp.repeat(normed, top_count, axis=0)
    outgoing = jnp.zeros((experts * capacity, model_width), jnp.bfloat16).at[target].set(repeated)
    outgoing = outgoing.reshape(experts, 1, capacity, model_width)
    hidden_width = w_down.shape[1]
    inner_act = jnp.einsum(
        "esmd,edf->esmf",
        lax.all_to_all(outgoing, "head", split_axis=0, concat_axis=1, tiled=True),
        w_in,
        preferred_element_type=jnp.float32,
    )
    hidden = (jax.nn.silu(inner_act[..., :hidden_width]) * inner_act[..., hidden_width:]).astype(
        jnp.bfloat16
    )
    answered = jnp.einsum(
        "esmf,efd->esmd", hidden, w_down, preferred_element_type=jnp.float32
    ).astype(jnp.bfloat16)
    returned_rows = lax.all_to_all(answered, "head", split_axis=1, concat_axis=0, tiled=True)
    picked = returned_rows.reshape(experts * capacity, model_width)[target].astype(jnp.float32)
    weighted = picked * expert_gates.reshape(-1)[:, None]
    expert_sum = weighted.reshape(row_count, top_count, model_width).sum(1)
    return (stream + expert_sum).astype(jnp.bfloat16).reshape(local_rows, seq_count, model_width)


def solution(mesh):
    return jax.shard_map(
        local,
        mesh=mesh,
        in_specs=(
            P("head", "grp", None, None),
            P("head", "grp", None, None),
            P(("grp", "head"), None, None),
            P("head", "grp", None),
            P(None, "head", None),
            P(),
            P("head", "grp", None),
            P("head", "grp", None),
            P("head", None, None),
            P("head", None, None),
        ),
        out_specs=P("head", "grp", None),
        check_vma=False,
    )
```

profile of v0, /device:TPU:15, one launch (start us, length us, event | category | flops | bytes accessed | tf_op | source)
XLA Modules:
  0.0 386.3 jit_solution(4581564289091582553)
XLA Ops:
  9.7 6.5 %all-to-all-start.1 = ((bf16[128,16,512]{2,0,1:T(8,128)(2,1)}), bf16[128,16,512]{2,0,1:T(8,128)(2,1)}, u32[]{:S(2)}, u32[]{:S(2)}) async-start(bf16[128,16,512]{2,0,1:T(8,128)(2,1)} %bitcast.108), calls=%async_computation.1 | async-start | bytes 4194304 | tf_op jit(solution)/shard_map/all_to_all | solution.py:69
  18.5 33.3 %collective-permute-done.1 = bf16[512,512]{1,0:T(8,128)(2,1)S(1)} collective-permute-done((bf16[512,512]{1,0:T(8,128)(2,1)S(1)}, bf16[512,512]{1,0:T(8,128)(2,1)S(1)}, u32[]{:S(2)}, u32[]{:S(2)}) %collective-permute-start.1) | collective-permute-done | bytes 524320 | tf_op jit(solution)/shard_map/ppermute | solution.py:12
  52.8 4.1 %collective-permute-start.2 = (bf16[1024,512]{1,0:T(8,128)(2,1)}, bf16[1024,512]{1,0:T(8,128)(2,1)}, u32[]{:S(2)}, u32[]{:S(2)}) collective-permute-start(bf16[1024,512]{1,0:T(8,128)(2,1)} %pad_maximum_fusion.1), channel_id=1, source_target_pairs={{0,4},{1,5},{2,6},{3,7},{4,0},{5,1},{6,2},{7,3},{8,12},{9,13},{10,... | collective-permute-start | bytes 3145736 | tf_op jit(solution)/shard_map/ppermute | solution.py:12
  56.9 2.6 copy.42
  59.5 38.3 %all-to-all-done.1 = bf16[128,16,512]{2,0,1:T(8,128)(2,1)} async-done(((bf16[128,16,512]{2,0,1:T(8,128)(2,1)}), bf16[128,16,512]{2,0,1:T(8,128)(2,1)}, u32[]{:S(2)}, u32[]{:S(2)}) %all-to-all-start.1) | async-done | bytes 2097184 | tf_op jit(solution)/shard_map/all_to_all | solution.py:69
  97.7 4.4 %all-to-all-start = ((bf16[128,16,256]{2,0,1:T(8,128)(2,1)}), bf16[128,16,256]{2,0,1:T(8,128)(2,1)}, u32[]{:S(2)}, u32[]{:S(2)}) async-start(bf16[128,16,256]{2,0,1:T(8,128)(2,1)} %bitcast.95), calls=%async_computation | async-start | bytes 2097152 | tf_op jit(solution)/shard_map/all_to_all | solution.py:66
  102.2 20.2 %collective-permute-done.2 = bf16[1024,512]{1,0:T(8,128)(2,1)} collective-permute-done((bf16[1024,512]{1,0:T(8,128)(2,1)}, bf16[1024,512]{1,0:T(8,128)(2,1)}, u32[]{:S(2)}, u32[]{:S(2)}) %collective-permute-start.2) | collective-permute-done | bytes 1048608 | tf_op jit(solution)/shard_map/ppermute | solution.py:12
  124.9 3.0 fusion.57
  128.0 24.3 %all-to-all-done = bf16[128,16,256]{2,0,1:T(8,128)(2,1)} async-done(((bf16[128,16,256]{2,0,1:T(8,128)(2,1)}), bf16[128,16,256]{2,0,1:T(8,128)(2,1)}, u32[]{:S(2)}, u32[]{:S(2)}) %all-to-all-start) | async-done | bytes 1048608 | tf_op jit(solution)/shard_map/all_to_all | solution.py:66
  152.3 45.5 %while.11 = (s32[]{:T(128)}, bf16[4,512,256]{2,1,0:T(8,128)(2,1)}, s32[4]{0:T(128)S(1)}, bf16[2048,256]{1,0:T(8,128)(2,1)}, bf16[2048,256]{1,0:T(8,128)(2,1)S(1)...) while((s32[]{:T(128)}, bf16[4,512,256]{2,1,0:T(8,128)(2,1)}, ...), condition=%wide.region_5.6_spmd.clone, body=%wide.region_0.5_spmd.clone.sunk | while | flops 2164653568 | bytes 39617248 | solution.py:48
  155.4 2.3 fusion.81
  166.8 2.3 fusion.81
  178.2 2.3 fusion.81
  180.5 1.8 multiply_reduce_fusion.4
  189.6 2.3 fusion.81
  191.8 1.8 multiply_reduce_fusion.4
  198.3 2.7 reduce.2
  202.1 4.8 %all-to-all-start.2 = ((bf16[16,2,16384]{2,1,0:T(2,128)(2,1)}), bf16[16,2,16384]{2,1,0:T(2,128)(2,1)S(1)}, u32[]{:S(2)}, u32[]{:S(2)}) async-start(bf16[16,2,16384]{2,1,0:T(2,128)(2,1)} %reshape.162), calls=%async_computation.2 | async-start | bytes 2097152 | tf_op jit(solution)/shard_map/all_to_all | solution.py:77
  208.5 23.3 %all-to-all-done.2 = bf16[16,2,16384]{2,1,0:T(2,128)(2,1)S(1)} async-done(((bf16[16,2,16384]{2,1,0:T(2,128)(2,1)}), bf16[16,2,16384]{2,1,0:T(2,128)(2,1)S(1)}, u32[]{:S(2)}, u32[]{:S(2)}) %all-to-all-start.2) | async-done | bytes 1048608 | tf_op jit(solution)/shard_map/all_to_all | solution.py:77
  231.8 3.5 reshape.163
  235.2 2.8 copy.38
  238.0 8.6 %multiply_reduce_fusion.2 = (f32[128]{0:T(128)S(1)}, f32[128,2048]{1,0:T(8,128)S(1)}) fusion(bf16[128,16,256]{2,0,1:T(8,128)(2,1)} %bitcast.110, bf16[16,256,2048]{2,1,0:T(8,128)(2,1)} %all-gather.2.cloned.1.call-done, bf16[128,1,2048]{2,0,1:T(8,128)(2,1)} %param.15), kind=kOutput, calls=%fused_computation.46 | convolution fusion | flops 2148532224 | bytes 19399168 | tf_op jit(solution)/shard_map/rhi,hid->rd/dot_general | solution.py:86
  248.4 2.3 reshape.152
  250.6 4.4 %scatter_custom_fusion = bf16[512,2048]{1,0:T(8,128)(2,1)} fusion(s32[256]{0:T(256)S(1)} %bitcast.116, bf16[256,2048]{1,0:T(8,128)(2,1)} %reshape.152, bf16[]{:T(256)} %constant.7.clone.1), kind=kCustom, calls=%fused_computation.47 | custom fusion | bytes 2097664 | tf_op jit(solution)/shard_map/scatter | solution.py:105
  255.1 52.4 %all_to_all.66 = bf16[16,1,32,2048]{3,2,1,0:T(8,128)(2,1)S(1)} all-to-all(bf16[16,1,32,2048]{3,2,1,0:T(8,128)(2,1)} %bitcast.109), channel_id=1, replica_groups=mesh['grp'=2,'head'=16] {'head'}, dimensions={0} | all-to-all | bytes 4194304 | tf_op jit(solution)/shard_map/all_to_all | solution.py:110
  307.4 2.3 fusion.40
  309.8 2.6 fusion.36
  312.4 5.2 %all-to-all-start.4 = ((bf16[1,16,32,2048]{3,2,0,1:T(8,128)(2,1)}), bf16[1,16,32,2048]{3,2,0,1:T(8,128)(2,1)}, u32[]{:S(2)}, u32[]{:S(2)}) async-start(bf16[1,16,32,2048]{3,2,0,1:T(8,128)(2,1)} %fusion.36), calls=%async_computation.4 | async-start | bytes 4194304 | tf_op jit(solution)/shard_map/all_to_all | solution.py:120
  317.7 47.4 %all-to-all-done.4 = bf16[1,16,32,2048]{3,2,0,1:T(8,128)(2,1)} async-done(((bf16[1,16,32,2048]{3,2,0,1:T(8,128)(2,1)}), bf16[1,16,32,2048]{3,2,0,1:T(8,128)(2,1)}, u32[]{:S(2)}, u32[]{:S(2)}) %all-to-all-start.4) | async-done | bytes 2097184 | tf_op jit(solution)/shard_map/all_to_all | solution.py:120
  365.1 5.2 %gather_fusion = bf16[256,2048]{1,0:T(8,128)(2,1)} fusion(bf16[512,2048]{1,0:T(8,128)(2,1)} %bitcast.30, s32[1024]{0:T(1024)S(1)} %pad_clamp_fusion), kind=kCustom, calls=%fused_computation | custom fusion | bytes 2098176 | tf_op jit(solution)/shard_map/gather | solution.py:121
  370.3 3.4 reshape.139
  373.7 4.8 %multiply_reduce_fusion.1 = f32[128,2048]{1,0:T(8,128)S(1)} fusion(f32[128,2,2048]{2,1,0:T(2,128)} %reshape.139, f32[128,2]{1,0:T(8,128)S(1)} %copy.37), kind=kLoop, calls=%fused_computation.38 | loop fusion | flops 786432 | bytes 3146752 | tf_op jit(solution)/shard_map/reduce_sum | solution.py:123
  (93 shorter events, 39.9 us)
Async XLA Ops:
  6.5 303.3 %copy-start = (bf16[1,512,2048]{2,1,0:T(8,128)(2,1)S(1)}, bf16[1,512,2048]{2,1,0:T(8,128)(2,1)}, u32[]{:S(2)}) copy-start(bf16[1,512,2048]{2,1,0:T(8,128)(2,1)} %param.21) | copy-start | bytes 6291460
  6.5 9.7 %copy-start.1 = (bf16[1,256,512]{2,1,0:T(8,128)(2,1)S(1)}, bf16[1,256,512]{2,1,0:T(8,128)(2,1)}, u32[]{:S(2)}) copy-start(bf16[1,256,512]{2,1,0:T(8,128)(2,1)} %param.14) | copy-start | bytes 786436
  6.5 231.4 %all-gather.2.cloned.1.call-start = ((), (), s32[]{:S(2)}) async-start(), calls=%async_computation.5 | async-start | bytes 17825792 | tf_op jit(solution)/shard_map/all_gather | solution.py:89
  9.7 88.0 %all-to-all-start.1 = ((bf16[128,16,512]{2,0,1:T(8,128)(2,1)}), bf16[128,16,512]{2,0,1:T(8,128)(2,1)}, u32[]{:S(2)}, u32[]{:S(2)}) async-start(bf16[128,16,512]{2,0,1:T(8,128)(2,1)} %bitcast.108), calls=%async_computation.1 | async-start | bytes 4194304 | tf_op jit(solution)/shard_map/all_to_all | solution.py:69
  16.3 1.8 collective-permute-start
  18.1 33.7 %collective-permute-start.1 = (bf16[512,512]{1,0:T(8,128)(2,1)S(1)}, bf16[512,512]{1,0:T(8,128)(2,1)S(1)}, u32[]{:S(2)}, u32[]{:S(2)}) collective-permute-start(bf16[512,512]{1,0:T(8,128)(2,1)S(1)} %pad_maximum_fusion.2), channel_id=1, source_target_pairs={{0,2},{1,3},{2,0},{3,1},{4,6},{5,7},{6,4},{7,5},{8,10},{9,11},{10,... | collective-permute-start | bytes 1572872 | tf_op jit(solution)/shard_map/ppermute | solution.py:12
  52.8 69.6 %collective-permute-start.2 = (bf16[1024,512]{1,0:T(8,128)(2,1)}, bf16[1024,512]{1,0:T(8,128)(2,1)}, u32[]{:S(2)}, u32[]{:S(2)}) collective-permute-start(bf16[1024,512]{1,0:T(8,128)(2,1)} %pad_maximum_fusion.1), channel_id=1, source_target_pairs={{0,4},{1,5},{2,6},{3,7},{4,0},{5,1},{6,2},{7,3},{8,12},{9,13},{10,... | collective-permute-start | bytes 3145736 | tf_op jit(solution)/shard_map/ppermute | solution.py:12
  97.7 54.5 %all-to-all-start = ((bf16[128,16,256]{2,0,1:T(8,128)(2,1)}), bf16[128,16,256]{2,0,1:T(8,128)(2,1)}, u32[]{:S(2)}, u32[]{:S(2)}) async-start(bf16[128,16,256]{2,0,1:T(8,128)(2,1)} %bitcast.95), calls=%async_computation | async-start | bytes 2097152 | tf_op jit(solution)/shard_map/all_to_all | solution.py:66
  159.5 1.4 copy-start.2
  160.9 1.2 copy-start.3
  170.9 1.4 copy-start.2
  172.3 1.2 copy-start.3
  182.3 1.4 copy-start.2
  183.7 1.2 copy-start.3
  193.7 1.4 copy-start.2
  195.1 1.2 copy-start.3
  197.8 9.1 %copy-start.5 = (s32[128,1,2]{0,2,1:T(2,128)S(1)}, s32[128,1,2]{0,2,1:T(2,128)}, u32[]{:S(2)}) copy-start(s32[128,1,2]{0,2,1:T(2,128)} %param.18) | copy-start | bytes 3076
  202.1 29.7 %all-to-all-start.2 = ((bf16[16,2,16384]{2,1,0:T(2,128)(2,1)}), bf16[16,2,16384]{2,1,0:T(2,128)(2,1)S(1)}, u32[]{:S(2)}, u32[]{:S(2)}) async-start(bf16[16,2,16384]{2,1,0:T(2,128)(2,1)} %reshape.162), calls=%async_computation.2 | async-start | bytes 2097152 | tf_op jit(solution)/shard_map/all_to_all | solution.py:77
  238.0 8.6 %copy-start.4 = (f32[2048]{0:T(1024)S(1)}, f32[2048]{0:T(1024)}, u32[]{:S(2)}) copy-start(f32[2048]{0:T(1024)} %param.17) | copy-start | bytes 24580
  255.1 52.4 %copy-start.7 = (bf16[1,2048,1024]{2,1,0:T(8,128)(2,1)S(1)}, bf16[1,2048,1024]{2,1,0:T(8,128)(2,1)}, u32[]{:S(2)}) copy-start(bf16[1,2048,1024]{2,1,0:T(8,128)(2,1)} %param.20) | copy-start | bytes 12582916
  312.4 5.2 %copy-start.6 = (f32[128,1,2]{0,2,1:T(2,128)S(1)}, f32[128,1,2]{0,2,1:T(2,128)}, u32[]{:S(2)}) copy-start(f32[128,1,2]{0,2,1:T(2,128)} %param.19) | copy-start | bytes 3076
  312.4 52.7 %all-to-all-start.4 = ((bf16[1,16,32,2048]{3,2,0,1:T(8,128)(2,1)}), bf16[1,16,32,2048]{3,2,0,1:T(8,128)(2,1)}, u32[]{:S(2)}, u32[]{:S(2)}) async-start(bf16[1,16,32,2048]{3,2,0,1:T(8,128)(2,1)} %fusion.36), calls=%async_computation.4 | async-start | bytes 4194304 | tf_op jit(solution)/shard_map/all_to_all | solution.py:120
Sparse Core Ops, SparseCore 0:
  9.5 185.4 all-gather.1
where the time goes:
time: 388 us; the launch traced here: 386 us
  waiting for transfers between devices  189 us (49%)
  blocking collectives  52.4 us (14%)
  matrix products  39.2 us (10%)
  local copies, waits for them, and re-layouts  38.8 us (10%)
  starting transfers between devices  25.8 us (7%)
  other arithmetic  19.9 us (5%)
  between operations  13.5 us (3%)
  loops' own time  7.86 us (2%)
    ppermute x3, waiting for transfers between devices, partner_2(): return lax.ppermute(value, axis, pairs)  54.9 us
    all_to_all x1, blocking collectives, local(): lax.all_to_all(outgoing, 'head', split_axis=0, concat_axis=1, tiled=True)  52.4 us
    all_to_all x1, waiting for transfers between devices, local(): lax.all_to_all(answered, 'head', split_axis=1, concat_axis=0, tiled=True)  47.4 us
    all_to_all x1, waiting for transfers between devices, local(): lax.all_to_all(pair_slots, 'head', split_axis=1, concat_axis=0, tiled=True)  38.3 us
    all_to_all x1, waiting for transfers between devices, local(): lax.all_to_all(query_slots, 'head', split_axis=1, concat_axis=0, tiled=True)  24.3 us
    all_to_all x1, waiting for transfers between devices, local(): lax.all_to_all(attended.reshape(attended.shape[0], 1, head_width), 'head'...  23.3 us
    unnamed x17, local copies, waits for them, and re-layouts  10 us
    dot_general x4, matrix products, one_block(): jnp.dot(query_rows, new_keys.T, preferred_element_type=jnp.float32)  9.17 us
  transfers between devices with their start and end apart: 8, of which 7 were waited for; matrix products, arithmetic and copies ran while one was open for 16% of the time, Pallas kernels for 0%

commit v1 on v0

--- a/solution.py
+++ b/solution.py
@@ -63,9 +63,12 @@
         new_kv[:, :, :, None, :], (local_rows, seq_count, pair_heads, group_size, 2 * head_width)
     )
     pair_slots = pair_slots.reshape(local_rows, axis_count, 2 * head_width)
-    head_queries = lax.all_to_all(query_slots, "head", split_axis=1, concat_axis=0, tiled=True)[
-        :, 0
-    ]
+    head_queries = jnp.concatenate(
+        lax.all_to_all(
+            jnp.stack(jnp.split(query_slots, lax.axis_size("head"), axis=1)), "head", 0, 0
+        ),
+        axis=0,
+    )[:, 0]
     head_pairs = lax.all_to_all(pair_slots, "head", split_axis=1, concat_axis=0, tiled=True)[:, 0]
     cache_rows = cache[0]
     for bit_number in range(group_size.bit_length() - 1):

time: 388 us -> 386 us (level)
  waiting for transfers between devices: 189 us -> 180 us
  local copies, waits for them, and re-layouts: 38.8 us -> 47.7 us
    ppermute x3, waiting for transfers between devices: 54.9 us -> 44.6 us  [partner_2(): return lax.ppermute(value, axis, pairs)]
    unnamed x17 -> x32, local copies, waits for them, and re-layouts: 10 us -> 18.4 us
  transfers between devices with their start and end apart: 8 -> 8, of which waited for: 7 -> 6; matrix products, arithmetic and copies ran while one was open for 16% -> 18% of each run, Pallas kernels for 0% -> 0%
where the time goes in v1:
time: 386 us; the launch traced here: 385 us
  waiting for transfers between devices  180 us (47%)
  blocking collectives  52.3 us (14%)
  local copies, waits for them, and re-layouts  47.7 us (12%)
  matrix products  39.1 us (10%)
  starting transfers between devices  25.8 us (7%)
  other arithmetic  19.6 us (5%)
  between operations  13.5 us (3%)
  loops' own time  6.95 us (2%)
    all_to_all x1, blocking collectives, local(): lax.all_to_all(outgoing, 'head', split_axis=0, concat_axis=1, tiled=True)  52.3 us
    all_to_all x1, waiting for transfers between devices, local(): lax.all_to_all(answered, 'head', split_axis=1, concat_axis=0, tiled=True)  47.4 us
    ppermute x3, waiting for transfers between devices, partner_2(): return lax.ppermute(value, axis, pairs)  44.6 us
    all_to_all x1, waiting for transfers between devices, local(): lax.all_to_all(pair_slots, 'head', split_axis=1, concat_axis=0, tiled=True)  39.6 us
    all_to_all x1, waiting for transfers between devices, local(): lax.all_to_all(jnp.stack(jnp.split(query_slots, lax.axis_size('head'), ax...  24.3 us
    all_to_all x1, waiting for transfers between devices, local(): lax.all_to_all(attended.reshape(attended.shape[0], 1, head_width), 'head'...  23.3 us
    unnamed x32, local copies, waits for them, and re-layouts  18.4 us
    dot_general x4, matrix products, one_block(): jnp.dot(query_rows, new_keys.T, preferred_element_type=jnp.float32)  9.17 us
  transfers between devices with their start and end apart: 8, of which 6 were waited for; matrix products, arithmetic and copies ran while one was open for 18% of the time, Pallas kernels for 0%

profile of v1, /device:TPU:15, one launch (start us, length us, event | category | flops | bytes accessed | tf_op | source)
XLA Modules:
  0.0 384.9 jit_solution(2189478793001961747)
XLA Ops:
  9.7 6.5 %all-to-all-start.1 = ((bf16[128,16,512]{2,0,1:T(8,128)(2,1)}), bf16[128,16,512]{2,0,1:T(8,128)(2,1)}, u32[]{:S(2)}, u32[]{:S(2)}) async-start(bf16[128,16,512]{2,0,1:T(8,128)(2,1)} %bitcast.168), calls=%async_computation.1 | async-start | bytes 4194304 | tf_op jit(solution)/shard_map/all_to_all | solution.py:72
  27.4 24.4 %collective-permute-done.1 = bf16[512,512]{1,0:T(8,128)(2,1)S(1)} collective-permute-done((bf16[512,512]{1,0:T(8,128)(2,1)S(1)}, bf16[512,512]{1,0:T(8,128)(2,1)S(1)}, u32[]{:S(2)}, u32[]{:S(2)}) %collective-permute-start.1) | collective-permute-done | bytes 524320 | tf_op jit(solution)/shard_map/ppermute | solution.py:12
  52.8 4.1 %collective-permute-start.2 = (bf16[1024,512]{1,0:T(8,128)(2,1)}, bf16[1024,512]{1,0:T(8,128)(2,1)}, u32[]{:S(2)}, u32[]{:S(2)}) collective-permute-start(bf16[1024,512]{1,0:T(8,128)(2,1)} %pad_maximum_fusion.1), channel_id=1, source_target_pairs={{0,4},{1,5},{2,6},{3,7},{4,0},{5,1},{6,2},{7,3},{8,12},{9,13},{10,... | collective-permute-start | bytes 3145736 | tf_op jit(solution)/shard_map/ppermute | solution.py:12
  58.2 39.6 %all-to-all-done.1 = bf16[128,16,512]{2,0,1:T(8,128)(2,1)} async-done(((bf16[128,16,512]{2,0,1:T(8,128)(2,1)}), bf16[128,16,512]{2,0,1:T(8,128)(2,1)}, u32[]{:S(2)}, u32[]{:S(2)}) %all-to-all-start.1) | async-done | bytes 2097184 | tf_op jit(solution)/shard_map/all_to_all | solution.py:72
  97.7 4.4 %all-to-all-start = ((bf16[16,128,1,256]{3,1,2,0:T(8,128)(2,1)}), bf16[16,128,1,256]{3,1,2,0:T(8,128)(2,1)}, u32[]{:S(2)}, u32[]{:S(2)}) async-start(bf16[16,128,1,256]{3,1,2,0:T(8,128)(2,1)} %fusion.51), calls=%async_computation | async-start | bytes 2097152 | tf_op jit(solution)/shard_map/all_to_all | solution.py:67
  102.2 20.2 %collective-permute-done.2 = bf16[1024,512]{1,0:T(8,128)(2,1)} collective-permute-done((bf16[1024,512]{1,0:T(8,128)(2,1)}, bf16[1024,512]{1,0:T(8,128)(2,1)}, u32[]{:S(2)}, u32[]{:S(2)}) %collective-permute-start.2) | collective-permute-done | bytes 1048608 | tf_op jit(solution)/shard_map/ppermute | solution.py:12
  124.9 3.0 fusion.73
  128.0 24.3 %all-to-all-done = bf16[16,128,1,256]{3,1,2,0:T(8,128)(2,1)} async-done(((bf16[16,128,1,256]{3,1,2,0:T(8,128)(2,1)}), bf16[16,128,1,256]{3,1,2,0:T(8,128)(2,1)}, u32[]{:S(2)}, u32[]{:S(2)}) %all-to-all-start) | async-done | bytes 1048608 | tf_op jit(solution)/shard_map/all_to_all | solution.py:67
  152.3 44.2 %while.11 = (s32[]{:T(128)}, bf16[4,512,256]{2,1,0:T(8,128)(2,1)}, s32[4]{0:T(128)S(1)}, bf16[2048,256]{1,0:T(8,128)(2,1)}, bf16[2048,256]{1,0:T(8,128)(2,1)S(1)...) while((s32[]{:T(128)}, bf16[4,512,256]{2,1,0:T(8,128)(2,1)}, ...), condition=%wide.region_5.6_spmd.clone, body=%wide.region_0.5_spmd.clone.sunk | while | flops 2164653568 | bytes 39617248 | solution.py:48
  155.1 2.3 fusion.97
  157.4 1.8 multiply_reduce_fusion.4
  166.1 2.3 fusion.97
  168.4 1.8 multiply_reduce_fusion.4
  177.2 2.3 fusion.97
  179.5 1.8 multiply_reduce_fusion.4
  188.2 2.3 fusion.97
  196.9 2.7 reduce.2
  200.7 4.8 %all-to-all-start.2 = ((bf16[16,2,16384]{2,1,0:T(2,128)(2,1)}), bf16[16,2,16384]{2,1,0:T(2,128)(2,1)S(1)}, u32[]{:S(2)}, u32[]{:S(2)}) async-start(bf16[16,2,16384]{2,1,0:T(2,128)(2,1)} %reshape.161), calls=%async_computation.2 | async-start | bytes 2097152 | tf_op jit(solution)/shard_map/all_to_all | solution.py:80
  207.2 23.3 %all-to-all-done.2 = bf16[16,2,16384]{2,1,0:T(2,128)(2,1)S(1)} async-done(((bf16[16,2,16384]{2,1,0:T(2,128)(2,1)}), bf16[16,2,16384]{2,1,0:T(2,128)(2,1)S(1)}, u32[]{:S(2)}, u32[]{:S(2)}) %all-to-all-start.2) | async-done | bytes 1048608 | tf_op jit(solution)/shard_map/all_to_all | solution.py:80
  230.4 3.5 reshape.162
  233.9 2.8 copy.52
  236.7 8.6 %multiply_reduce_fusion.2 = (f32[128]{0:T(128)S(1)}, f32[128,2048]{1,0:T(8,128)S(1)}) fusion(bf16[128,16,256]{2,0,1:T(8,128)(2,1)} %bitcast.170, bf16[16,256,2048]{2,1,0:T(8,128)(2,1)} %all-gather.2.cloned.1.call-done, bf16[128,1,2048]{2,0,1:T(8,128)(2,1)} %param.15), kind=kOutput, calls=%fused_computation.46 | convolution fusion | flops 2148532224 | bytes 19399168 | tf_op jit(solution)/shard_map/rhi,hid->rd/dot_general | solution.py:89
  247.1 2.3 reshape.151
  249.3 4.4 %scatter_custom_fusion = bf16[512,2048]{1,0:T(8,128)(2,1)} fusion(s32[256]{0:T(256)S(1)} %bitcast.192, bf16[256,2048]{1,0:T(8,128)(2,1)} %reshape.151, bf16[]{:T(256)} %constant.7.clone.1), kind=kCustom, calls=%fused_computation.47 | custom fusion | bytes 2097664 | tf_op jit(solution)/shard_map/scatter | solution.py:108
  253.7 52.3 %all_to_all.56 = bf16[16,1,32,2048]{3,2,1,0:T(8,128)(2,1)S(1)} all-to-all(bf16[16,1,32,2048]{3,2,1,0:T(8,128)(2,1)} %bitcast.169), channel_id=1, replica_groups=mesh['grp'=2,'head'=16] {'head'}, dimensions={0} | all-to-all | bytes 4194304 | tf_op jit(solution)/shard_map/all_to_all | solution.py:113
  306.1 2.3 fusion.40
  308.4 2.6 fusion.36
  311.0 5.2 %all-to-all-start.4 = ((bf16[1,16,32,2048]{3,2,0,1:T(8,128)(2,1)}), bf16[1,16,32,2048]{3,2,0,1:T(8,128)(2,1)}, u32[]{:S(2)}, u32[]{:S(2)}) async-start(bf16[1,16,32,2048]{3,2,0,1:T(8,128)(2,1)} %fusion.36), calls=%async_computation.4 | async-start | bytes 4194304 | tf_op jit(solution)/shard_map/all_to_all | solution.py:123
  316.3 47.4 %all-to-all-done.4 = bf16[1,16,32,2048]{3,2,0,1:T(8,128)(2,1)} async-done(((bf16[1,16,32,2048]{3,2,0,1:T(8,128)(2,1)}), bf16[1,16,32,2048]{3,2,0,1:T(8,128)(2,1)}, u32[]{:S(2)}, u32[]{:S(2)}) %all-to-all-start.4) | async-done | bytes 2097184 | tf_op jit(solution)/shard_map/all_to_all | solution.py:123
  363.7 5.2 %gather_fusion = bf16[256,2048]{1,0:T(8,128)(2,1)} fusion(bf16[512,2048]{1,0:T(8,128)(2,1)} %bitcast.44, s32[1024]{0:T(1024)S(1)} %pad_clamp_fusion), kind=kCustom, calls=%fused_computation | custom fusion | bytes 2098176 | tf_op jit(solution)/shard_map/gather | solution.py:124
  368.9 3.4 reshape.138
  372.3 4.8 %multiply_reduce_fusion.1 = f32[128,2048]{1,0:T(8,128)S(1)} fusion(f32[128,2,2048]{2,1,0:T(2,128)} %reshape.138, f32[128,2]{1,0:T(8,128)S(1)} %copy.51), kind=kLoop, calls=%fused_computation.38 | loop fusion | flops 786432 | bytes 3146752 | tf_op jit(solution)/shard_map/reduce_sum | solution.py:126
  (109 shorter events, 47.8 us)
Async XLA Ops:
  6.5 301.9 %copy-start = (bf16[1,512,2048]{2,1,0:T(8,128)(2,1)S(1)}, bf16[1,512,2048]{2,1,0:T(8,128)(2,1)}, u32[]{:S(2)}) copy-start(bf16[1,512,2048]{2,1,0:T(8,128)(2,1)} %param.21) | copy-start | bytes 6291460
  6.5 9.7 %copy-start.1 = (bf16[1,256,512]{2,1,0:T(8,128)(2,1)S(1)}, bf16[1,256,512]{2,1,0:T(8,128)(2,1)}, u32[]{:S(2)}) copy-start(bf16[1,256,512]{2,1,0:T(8,128)(2,1)} %param.14) | copy-start | bytes 786436
  6.5 230.1 %all-gather.2.cloned.1.call-start = ((), (), s32[]{:S(2)}) async-start(), calls=%async_computation.5 | async-start | bytes 17825792 | tf_op jit(solution)/shard_map/all_gather | solution.py:92
  9.7 88.0 %all-to-all-start.1 = ((bf16[128,16,512]{2,0,1:T(8,128)(2,1)}), bf16[128,16,512]{2,0,1:T(8,128)(2,1)}, u32[]{:S(2)}, u32[]{:S(2)}) async-start(bf16[128,16,512]{2,0,1:T(8,128)(2,1)} %bitcast.168), calls=%async_computation.1 | async-start | bytes 4194304 | tf_op jit(solution)/shard_map/all_to_all | solution.py:72
  16.3 8.9 %collective-permute-start = (bf16[256,512]{1,0:T(8,128)(2,1)S(1)}, bf16[256,512]{1,0:T(8,128)(2,1)S(1)}, u32[]{:S(2)}, u32[]{:S(2)}) collective-permute-start(bf16[256,512]{1,0:T(8,128)(2,1)S(1)} %bitcast.187), channel_id=1, source_target_pairs={{0,1},{1,0},{2,3},{3,2},{4,5},{5,4},{6,7},{7,6},{8,9},{9,8},{10,11... | collective-permute-start | bytes 786440 | tf_op jit(solution)/shard_map/ppermute | solution.py:12
  25.2 26.6 %collective-permute-start.1 = (bf16[512,512]{1,0:T(8,128)(2,1)S(1)}, bf16[512,512]{1,0:T(8,128)(2,1)S(1)}, u32[]{:S(2)}, u32[]{:S(2)}) collective-permute-start(bf16[512,512]{1,0:T(8,128)(2,1)S(1)} %pad_maximum_fusion.2), channel_id=1, source_target_pairs={{0,2},{1,3},{2,0},{3,1},{4,6},{5,7},{6,4},{7,5},{8,10},{9,11},{10,... | collective-permute-start | bytes 1572872 | tf_op jit(solution)/shard_map/ppermute | solution.py:12
  52.8 69.6 %collective-permute-start.2 = (bf16[1024,512]{1,0:T(8,128)(2,1)}, bf16[1024,512]{1,0:T(8,128)(2,1)}, u32[]{:S(2)}, u32[]{:S(2)}) collective-permute-start(bf16[1024,512]{1,0:T(8,128)(2,1)} %pad_maximum_fusion.1), channel_id=1, source_target_pairs={{0,4},{1,5},{2,6},{3,7},{4,0},{5,1},{6,2},{7,3},{8,12},{9,13},{10,... | collective-permute-start | bytes 3145736 | tf_op jit(solution)/shard_map/ppermute | solution.py:12
  97.7 54.5 %all-to-all-start = ((bf16[16,128,1,256]{3,1,2,0:T(8,128)(2,1)}), bf16[16,128,1,256]{3,1,2,0:T(8,128)(2,1)}, u32[]{:S(2)}, u32[]{:S(2)}) async-start(bf16[16,128,1,256]{3,1,2,0:T(8,128)(2,1)} %fusion.51), calls=%async_computation | async-start | bytes 2097152 | tf_op jit(solution)/shard_map/all_to_all | solution.py:67
  159.2 1.4 copy-start.2
  160.6 1.2 copy-start.3
  170.2 1.4 copy-start.2
  171.6 1.2 copy-start.3
  181.3 1.4 copy-start.2
  182.6 1.2 copy-start.3
  192.3 1.4 copy-start.2
  193.7 1.2 copy-start.3
  196.4 9.2 %copy-start.5 = (s32[128,1,2]{0,2,1:T(2,128)S(1)}, s32[128,1,2]{0,2,1:T(2,128)}, u32[]{:S(2)}) copy-start(s32[128,1,2]{0,2,1:T(2,128)} %param.18) | copy-start | bytes 3076
  200.7 29.7 %all-to-all-start.2 = ((bf16[16,2,16384]{2,1,0:T(2,128)(2,1)}), bf16[16,2,16384]{2,1,0:T(2,128)(2,1)S(1)}, u32[]{:S(2)}, u32[]{:S(2)}) async-start(bf16[16,2,16384]{2,1,0:T(2,128)(2,1)} %reshape.161), calls=%async_computation.2 | async-start | bytes 2097152 | tf_op jit(solution)/shard_map/all_to_all | solution.py:80
  236.7 8.6 %copy-start.4 = (f32[2048]{0:T(1024)S(1)}, f32[2048]{0:T(1024)}, u32[]{:S(2)}) copy-start(f32[2048]{0:T(1024)} %param.17) | copy-start | bytes 24580
  253.7 52.3 %copy-start.7 = (bf16[1,2048,1024]{2,1,0:T(8,128)(2,1)S(1)}, bf16[1,2048,1024]{2,1,0:T(8,128)(2,1)}, u32[]{:S(2)}) copy-start(bf16[1,2048,1024]{2,1,0:T(8,128)(2,1)} %param.20) | copy-start | bytes 12582916
  311.0 5.2 %copy-start.6 = (f32[128,1,2]{0,2,1:T(2,128)S(1)}, f32[128,1,2]{0,2,1:T(2,128)}, u32[]{:S(2)}) copy-start(f32[128,1,2]{0,2,1:T(2,128)} %param.19) | copy-start | bytes 3076
  311.0 52.7 %all-to-all-start.4 = ((bf16[1,16,32,2048]{3,2,0,1:T(8,128)(2,1)}), bf16[1,16,32,2048]{3,2,0,1:T(8,128)(2,1)}, u32[]{:S(2)}, u32[]{:S(2)}) async-start(bf16[1,16,32,2048]{3,2,0,1:T(8,128)(2,1)} %fusion.36), calls=%async_computation.4 | async-start | bytes 4194304 | tf_op jit(solution)/shard_map/all_to_all | solution.py:123
Sparse Core Ops, SparseCore 0:
  9.5 185.4 all-gather.1
